TPU v7x, 32 devices: a whole 2x2x4 slice. The times are simulated.
32 devices in a mesh: rep: 2 (over core), grp: 16 (over z, y, x).
Axes of the slice: x: 2, y: 2, z: 4, core: 2. Of those that a mesh axis runs over, the one named last changes fastest.
Arguments:
- grad_parts: float32 [2, 1024, 9216], P('rep', 'grp'), may hold values from -6 to 6
- gain_grad_parts: float32 [2, 2, 1024], P('rep', None, 'grp'), may hold values from -6 to 6
- weights: float32 [1024, 9216], P('grp'), may hold values from -0.1875 to 0.1875
- basis: float32 [1024, 256], P('grp'), may hold values from -0.1875 to 0.1875
- moment_first: float32 [9216, 256], P('grp'), may hold values from -12 to 12
- moment_second: float32 [9216, 256], P('grp'), may hold values from 0.01 to 1
- gains: float32 [2, 1024], P(None, 'grp'), may hold values from 0.5 to 1.5
- gain_first: float32 [2, 1024], P(None, 'grp'), may hold values from -12 to 12
- gain_second: float32 [2, 1024], P(None, 'grp'), may hold values from 0.01 to 1
Outputs:
- new_weights: float32 [1024, 9216], P('grp')
- new_first: float32 [9216, 256], P('grp')
- new_second: float32 [9216, 256], P('grp')
- new_basis: float32 [1024, 256], P('grp')
- new_gains: float32 [2, 1024], P(None, 'grp')
- new_gain_first: float32 [2, 1024], P(None, 'grp')
- new_gain_second: float32 [2, 1024], P(None, 'grp')
All inputs are finite; a program needn't handle non-finite values.
Results may differ from a plain program's by a relative error of at most 0.0001.
Values sent between devices are 32-bit elements; how exact they have to be, the bound alone decides.
A program may use at most 64 MiB of HBM per device.

v0:
```python
import jax
import jax.numpy as jnp
from jax import lax
from jax.sharding import PartitionSpec as P

NS_STEPS = 3
beta_first = 0.9
beta_second = 0.999
learn_rate = 0.1
galore_scale = 0.25
adam_eps = 1e-08


def exact_dot(left, right):
    return jnp.dot(left, right, precision=lax.Precision.HIGHEST, preferred_element_type=jnp.float32)


def body(
    grad_parts,
    gain_grad_parts,
    weights,
    basis,
    moment_first,
    moment_second,
    gains,
    gain_first,
    gain_second,
):
    corr_first = 1.0 - beta_first**10
    corr_second = 1.0 - beta_second**10
    n = lax.axis_size("grp")
    rep = lax.axis_index("rep")
    swap = [(0, 1), (1, 0)]
    local_grad = grad_parts[0]
    local_gain = gain_grad_parts[0]
    rows, ncol = local_grad.shape
    half = rows // 2
    block = ncol // n
    rank = basis.shape[1]

    def own_half(x):
        return lax.dynamic_slice_in_dim(x, rep * half, half, 0)

    def other_half(x):
        return lax.dynamic_slice_in_dim(x, (1 - rep) * half, half, 0)

    def swapped(x):
        return lax.ppermute(x, "rep", swap)

    def joined(mine, other):
        return jnp.where(
            rep == 0, jnp.concatenate([mine, other], 0), jnp.concatenate([other, mine], 0)
        )

    def exchange(x):
        return lax.all_to_all(x, "grp", split_axis=0, concat_axis=0, tiled=True)

    def gathered(x):
        return exchange(jnp.tile(x, (n, 1)))

    half_basis = gathered(own_half(basis))
    source = own_half(local_grad) + swapped(other_half(local_grad))
    gain_grad = local_gain + swapped(local_gain)
    col_block = lax.all_to_all(source, "grp", split_axis=1, concat_axis=0, tiled=True)
    partial = exact_dot(col_block.T, half_basis)
    projected = partial + swapped(partial)
    new_first = beta_first * moment_first + (1.0 - beta_first) * projected
    new_second = beta_second * moment_second + (1.0 - beta_second) * projected * projected
    direction = new_first / corr_first / (jnp.sqrt(new_second / corr_second) + adam_eps)
    terms = exchange(exact_dot(col_block, projected))
    sub_half = jnp.sum(terms.reshape(n, half, rank), axis=0)
    sub_all = gathered(sub_half)
    gram_half = exact_dot(sub_all.T, sub_all)
    gram = gram_half + swapped(gram_half)
    subspace = joined(sub_half, swapped(sub_half))
    update_cols = exact_dot(half_basis, direction.T)
    update = lax.all_to_all(update_cols, "grp", split_axis=0, concat_axis=1, tiled=True)
    new_half = own_half(weights) - learn_rate * galore_scale * update
    new_weights = joined(new_half, swapped(new_half))
    scale = jnp.sqrt(jnp.sqrt(jnp.sum(gram * gram) + 1e-06))
    iterate = subspace / scale
    current = gram / scale / scale
    for step in range(NS_STEPS):
        iterate = 1.5 * iterate - 0.5 * exact_dot(iterate, current)
        if step + 1 < NS_STEPS:
            side = 1.5 * current - 0.5 * exact_dot(current, current)
            current = 1.5 * side - 0.5 * exact_dot(side, current)
    new_gain_first = beta_first * gain_first + (1.0 - beta_first) * gain_grad
    new_gain_second = beta_second * gain_second + (1.0 - beta_second) * gain_grad * gain_grad
    new_gains = gains - learn_rate * (new_gain_first / corr_first) / (
        jnp.sqrt(new_gain_second / corr_second) + adam_eps
    )
    return (new_weights, new_first, new_second, iterate, new_gains, new_gain_first, new_gain_second)


def solution(mesh):
    in_specs = (
        P("rep", "grp", None),
        P("rep", None, "grp"),
        P("grp", None),
        P("grp", None),
        P("grp", None),
        P("grp", None),
        P(None, "grp"),
        P(None, "grp"),
        P(None, "grp"),
    )
    out_specs = (
        P("grp", None),
        P("grp", None),
        P("grp", None),
        P("grp", None),
        P(None, "grp"),
        P(None, "grp"),
        P(None, "grp"),
    )
    return jax.shard_map(body, mesh=mesh, in_specs=in_specs, out_specs=out_specs, check_vma=False)
```

profile of v0, /device:TPU:9, one launch (start us, length us, event | category | flops | bytes accessed | tf_op | source)
XLA Modules:
  0.0 149.2 jit_solution(4049808414563732338)
XLA Ops:
  0.6 0.0 copy-start
  0.7 1.4 dynamic-slice_bitcast_fusion
  2.0 0.7 collective-permute-start
  2.8 0.8 tile.4
  3.6 6.7 %all-to-all-start = ((f32[16,32,256]{2,1,0:T(8,128)}), f32[16,32,256]{2,1,0:T(8,128)S(1)}, u32[]{:S(2)}, u32[]{:S(2)}) async-start(f32[16,32,256]{2,1,0:T(8,128)} %tile.4), calls=%async_computation | async-start | bytes 1048576 | tf_op jit(solution)/shard_map/all_to_all | solution.py:56
  10.3 1.4 bitcast_add_fusion
  11.7 0.4 all_to_all.33
  12.2 0.4 copy.16
  12.6 11.6 %all-to-all-done = f32[16,32,256]{2,1,0:T(8,128)S(1)} async-done(((f32[16,32,256]{2,1,0:T(8,128)}), f32[16,32,256]{2,1,0:T(8,128)S(1)}, u32[]{:S(2)}, u32[]{:S(2)}) %all-to-all-start) | async-done | bytes 524320 | tf_op jit(solution)/shard_map/all_to_all | solution.py:56
  24.2 35.0 %all_to_all.44 = f32[32,16,576]{2,0,1:T(8,128)S(1)} all-to-all(f32[32,16,576]{2,0,1:T(8,128)S(1)} %copy.16), channel_id=1, replica_groups=mesh['rep'=2,'grp'=16] {'grp'}, dimensions={1} | all-to-all | bytes 2359296 | tf_op jit(solution)/shard_map/all_to_all | solution.py:64
  59.2 2.2 %fusion.4 = f32[576,256]{1,0:T(8,128)S(1)} fusion(f32[16,32,256]{2,1,0:T(8,128)S(1)} %all-to-all-done, f32[32,16,576]{2,0,1:T(8,128)S(1)} %all_to_all.44), kind=kOutput, calls=%fused_computation.6 | convolution fusion | flops 905969664 | bytes 2293760 | tf_op jit(solution)/shard_map/dot_general | solution.py:15
  61.5 2.0 %collective-permute-start.1 = (f32[576,256]{1,0:T(8,128)S(1)}, f32[576,256]{1,0:T(8,128)S(1)}, u32[]{:S(2)}, u32[]{:S(2)}) collective-permute-start(f32[576,256]{1,0:T(8,128)S(1)} %fusion.4), channel_id=1, source_target_pairs={{0,16},{16,0},{1,17},{17,1},{2,18},{18,2},{3,19},{19,3},{4,20},{20... | collective-permute-start | bytes 1769480 | tf_op jit(solution)/shard_map/ppermute | solution.py:48
  63.5 1.6 %collective-permute-done.1 = f32[576,256]{1,0:T(8,128)S(1)} collective-permute-done((f32[576,256]{1,0:T(8,128)S(1)}, f32[576,256]{1,0:T(8,128)S(1)}, u32[]{:S(2)}, u32[]{:S(2)}) %collective-permute-start.1) | collective-permute-done | bytes 589856 | tf_op jit(solution)/shard_map/ppermute | solution.py:48
  65.1 1.4 fusion
  66.5 17.3 %all_to_all.45 = f32[16,32,256]{2,1,0:T(8,128)S(1)} all-to-all(f32[16,32,256]{2,1,0:T(8,128)S(1)} %fusion), channel_id=1, replica_groups=mesh['rep'=2,'grp'=16] {'grp'}, dimensions={0} | all-to-all | bytes 1048576 | tf_op jit(solution)/shard_map/all_to_all | solution.py:56
  83.9 0.8 tile.5
  84.7 4.6 %all-to-all-start.4 = ((f32[16,32,256]{2,1,0:T(8,128)}), f32[16,32,256]{2,1,0:T(8,128)}, u32[]{:S(2)}, u32[]{:S(2)}) async-start(f32[16,32,256]{2,1,0:T(8,128)} %tile.5), calls=%async_computation.4 | async-start | bytes 1048576 | tf_op jit(solution)/shard_map/all_to_all | solution.py:56
  89.4 0.0 copy-start.4
  89.4 1.3 multiply_add_fusion
  90.7 0.0 copy-start.2
  90.7 0.0 copy-start.1
  90.7 0.8 copy-done.2
  91.5 2.7 %fusion.13 = f32[16,32,576]{2,1,0:T(8,128)} fusion(f32[16,32,256]{2,1,0:T(8,128)S(1)} %copy-done.4, f32[576,256]{1,0:T(8,128)S(1)} %get-tuple-element.13, f32[576,256]{1,0:T(8,128)S(1)} %get-tuple-element.12), kind=kOutput, calls=%fused_computation.25 | convolution fusion | flops 906559488 | bytes 2883584 | tf_op jit(solution)/shard_map/dot_general | solution.py:15
  94.3 0.0 copy-start.9
  94.3 8.3 %all-to-all-done.4 = f32[16,32,256]{2,1,0:T(8,128)} async-done(((f32[16,32,256]{2,1,0:T(8,128)}), f32[16,32,256]{2,1,0:T(8,128)}, u32[]{:S(2)}, u32[]{:S(2)}) %all-to-all-start.4) | async-done | bytes 524320 | tf_op jit(solution)/shard_map/all_to_all | solution.py:56
  102.6 5.1 %all-to-all-start.2 = ((f32[16,32,576]{2,1,0:T(8,128)}), f32[16,32,576]{2,1,0:T(8,128)S(1)}, u32[]{:S(2)}, u32[]{:S(2)}) async-start(f32[16,32,576]{2,1,0:T(8,128)} %fusion.13), calls=%async_computation.2 | async-start | bytes 2621440 | tf_op jit(solution)/shard_map/all_to_all | solution.py:77
  107.6 2.2 %collective-permute-start.5 = (f32[2,64]{1,0:T(2,128)S(1)}, f32[2,64]{1,0:T(2,128)S(1)}, u32[]{:S(2)}, u32[]{:S(2)}) collective-permute-start(f32[2,64]{1,0:T(2,128)S(1)} %bitcast.39), channel_id=1, source_target_pairs={{0,16},{16,0},{1,17},{17,1},{2,18},{18,2},{3,19},{19,3},{4,20},{20... | collective-permute-start | bytes 1544 | tf_op jit(solution)/shard_map/ppermute | solution.py:48
  109.8 0.8 collective-permute-done.5
  110.6 0.6 divide_subtract_fusion
  111.2 0.3 collective-permute-start.3
  111.6 2.2 %convolution_bitcast_fusion = f32[256,256]{1,0:T(8,128)S(1)} fusion(f32[16,32,256]{2,1,0:T(8,128)} %all-to-all-done.4), kind=kOutput, calls=%fused_computation.16 | convolution fusion | flops 402653184 | bytes 786432 | tf_op jit(solution)/shard_map/dot_general | solution.py:15
  113.8 0.2 collective-permute-start.4
  114.0 23.7 %all-to-all-done.2 = f32[16,32,576]{2,1,0:T(8,128)S(1)} async-done(((f32[16,32,576]{2,1,0:T(8,128)}), f32[16,32,576]{2,1,0:T(8,128)S(1)}, u32[]{:S(2)}, u32[]{:S(2)}) %all-to-all-start.2) | async-done | bytes 1179680 | tf_op jit(solution)/shard_map/all_to_all | solution.py:77
  137.8 0.1 multiply_bitcast_fusion
  137.9 0.8 copy.17
  138.7 0.5 mul.135
  139.1 1.4 dynamic-slice_subtract_fusion
  140.5 2.6 %collective-permute-start.2 = (f32[32,9216]{1,0:T(8,128)S(1)}, f32[32,9216]{1,0:T(8,128)S(1)}, u32[]{:S(2)}, u32[]{:S(2)}) collective-permute-start(f32[32,9216]{1,0:T(8,128)S(1)} %dynamic-slice_subtract_fusion), channel_id=1, source_target_pairs={{0,16},{16,0},{1,17},{17,1},{2,18},{18,2},{3,19},{19,3},{4,20},{20... | collective-permute-start | bytes 3538952 | tf_op jit(solution)/shard_map/ppermute | solution.py:48
  143.2 0.7 multiply_reduce_fusion
  144.6 0.4 convolution_multiply_fusion.3
  145.0 0.4 multiply_subtract_fusion
  145.4 0.0 collective-permute-done.3
  145.4 0.3 convolution_multiply_fusion.6
  145.7 0.3 fusion.10
  145.9 0.4 fusion.8
  146.3 0.4 fusion.7
  146.7 0.9 fusion.9
  147.6 1.6 %maximum_select_fusion = f32[64,9216]{1,0:T(8,128)} fusion(f32[32,9216]{1,0:T(8,128)S(1)} %collective-permute-done.2, f32[32,9216]{1,0:T(8,128)S(1)} %dynamic-slice_subtract_fusion, pred[]{:T(512)S(6)} %eq.4), kind=kLoop, calls=%fused_computation | loop fusion | flops 1769472 | bytes 4718593 | tf_op jit(solution)/shard_map/jit(_where)/select_n | solution.py:51
  (19 shorter events, 0.1 us)
Async XLA Ops:
  0.6 2.2 %copy-start = (f32[64,256]{1,0:T(8,128)S(1)}, f32[64,256]{1,0:T(8,128)}, u32[]{:S(2)}) copy-start(f32[64,256]{1,0:T(8,128)} %param.12) | copy-start | bytes 196612
  2.0 8.3 %collective-permute-start = (f32[32,9216]{1,0:T(8,128)S(1)}, f32[32,9216]{1,0:T(8,128)S(1)}, u32[]{:S(2)}, u32[]{:S(2)}) collective-permute-start(f32[32,9216]{1,0:T(8,128)S(1)} %dynamic-slice_bitcast_fusion), channel_id=1, source_target_pairs={{0,16},{16,0},{1,17},{17,1},{2,18},{18,2},{3,19},{19,3},{4,20},{20... | collective-permute-start | bytes 3538952 | tf_op jit(solution)/shard_map/ppermute | solution.py:48
  3.6 20.6 %all-to-all-start = ((f32[16,32,256]{2,1,0:T(8,128)}), f32[16,32,256]{2,1,0:T(8,128)S(1)}, u32[]{:S(2)}, u32[]{:S(2)}) async-start(f32[16,32,256]{2,1,0:T(8,128)} %tile.4), calls=%async_computation | async-start | bytes 1048576 | tf_op jit(solution)/shard_map/all_to_all | solution.py:56
  24.2 35.0 %copy-start.3 = (f32[16,32,256]{2,1,0:T(8,128)}, f32[16,32,256]{2,1,0:T(8,128)S(1)}, u32[]{:S(2)}) copy-start(f32[16,32,256]{2,1,0:T(8,128)S(1)} %all-to-all-done) | copy-start | bytes 1572868
  61.5 3.6 %collective-permute-start.1 = (f32[576,256]{1,0:T(8,128)S(1)}, f32[576,256]{1,0:T(8,128)S(1)}, u32[]{:S(2)}, u32[]{:S(2)}) collective-permute-start(f32[576,256]{1,0:T(8,128)S(1)} %fusion.4), channel_id=1, source_target_pairs={{0,16},{16,0},{1,17},{17,1},{2,18},{18,2},{3,19},{19,3},{4,20},{20... | collective-permute-start | bytes 1769480 | tf_op jit(solution)/shard_map/ppermute | solution.py:48
  83.8 5.5 %copy-start.5 = (f32[576,256]{1,0:T(8,128)S(1)}, f32[576,256]{1,0:T(8,128)}, u32[]{:S(2)}) copy-start(f32[576,256]{1,0:T(8,128)} %param.13) | copy-start | bytes 1769476
  84.7 17.9 %all-to-all-start.4 = ((f32[16,32,256]{2,1,0:T(8,128)}), f32[16,32,256]{2,1,0:T(8,128)}, u32[]{:S(2)}, u32[]{:S(2)}) async-start(f32[16,32,256]{2,1,0:T(8,128)} %tile.5), calls=%async_computation.4 | async-start | bytes 1048576 | tf_op jit(solution)/shard_map/all_to_all | solution.py:56
  89.4 2.2 %copy-start.4 = (f32[16,32,256]{2,1,0:T(8,128)S(1)}, f32[16,32,256]{2,1,0:T(8,128)}, u32[]{:S(2)}) copy-start(f32[16,32,256]{2,1,0:T(8,128)} %copy-done.3) | copy-start | bytes 1572868
  90.7 0.8 copy-start.2
  90.7 3.6 %copy-start.1 = (f32[576,256]{1,0:T(8,128)}, f32[576,256]{1,0:T(8,128)S(1)}, u32[]{:S(2)}) copy-start(f32[576,256]{1,0:T(8,128)S(1)} %get-tuple-element.12) | copy-start | bytes 1769476
  94.3 13.4 %copy-start.7 = (f32[1,2,64]{2,1,0:T(2,128)S(1)}, f32[1,2,64]{2,1,0:T(2,128)}, u32[]{:S(2)}) copy-start(f32[1,2,64]{2,1,0:T(2,128)} %param.10) | copy-start | bytes 1540
  94.3 16.4 %copy-start.6 = (f32[2,64]{1,0:T(2,128)S(1)}, f32[2,64]{1,0:T(2,128)}, u32[]{:S(2)}) copy-start(f32[2,64]{1,0:T(2,128)} %param.15) | copy-start | bytes 1540
  94.3 16.4 %copy-start.8 = (f32[2,64]{1,0:T(2,128)S(1)}, f32[2,64]{1,0:T(2,128)}, u32[]{:S(2)}) copy-start(f32[2,64]{1,0:T(2,128)} %param.16) | copy-start | bytes 1540
  94.3 16.4 %copy-start.9 = (f32[2,64]{1,0:T(2,128)S(1)}, f32[2,64]{1,0:T(2,128)}, u32[]{:S(2)}) copy-start(f32[2,64]{1,0:T(2,128)} %param.17) | copy-start | bytes 1540
  102.6 35.2 %all-to-all-start.2 = ((f32[16,32,576]{2,1,0:T(8,128)}), f32[16,32,576]{2,1,0:T(8,128)S(1)}, u32[]{:S(2)}, u32[]{:S(2)}) async-start(f32[16,32,576]{2,1,0:T(8,128)} %fusion.13), calls=%async_computation.2 | async-start | bytes 2621440 | tf_op jit(solution)/shard_map/all_to_all | solution.py:77
  107.6 3.0 %collective-permute-start.5 = (f32[2,64]{1,0:T(2,128)S(1)}, f32[2,64]{1,0:T(2,128)S(1)}, u32[]{:S(2)}, u32[]{:S(2)}) collective-permute-start(f32[2,64]{1,0:T(2,128)S(1)} %bitcast.39), channel_id=1, source_target_pairs={{0,16},{16,0},{1,17},{17,1},{2,18},{18,2},{3,19},{19,3},{4,20},{20... | collective-permute-start | bytes 1544 | tf_op jit(solution)/shard_map/ppermute | solution.py:48
  111.2 34.2 %collective-permute-start.3 = (f32[32,256]{1,0:T(8,128)S(1)}, f32[32,256]{1,0:T(8,128)S(1)}, u32[]{:S(2)}, u32[]{:S(2)}) collective-permute-start(f32[32,256]{1,0:T(8,128)S(1)} %reduce_sum.18), channel_id=1, source_target_pairs={{0,16},{16,0},{1,17},{17,1},{2,18},{18,2},{3,19},{19,3},{4,20},{20... | collective-permute-start | bytes 98312 | tf_op jit(solution)/shard_map/ppermute | solution.py:48
  113.8 29.4 %collective-permute-start.4 = (f32[256,256]{1,0:T(8,128)S(1)}, f32[256,256]{1,0:T(8,128)S(1)}, u32[]{:S(2)}, u32[]{:S(2)}) collective-permute-start(f32[256,256]{1,0:T(8,128)S(1)} %convolution_bitcast_fusion), channel_id=1, source_target_pairs={{0,16},{16,0},{1,17},{17,1},{2,18},{18,2},{3,19},{19,3},{4,20},{20... | collective-permute-start | bytes 786440 | tf_op jit(solution)/shard_map/ppermute | solution.py:48
  140.5 7.1 %collective-permute-start.2 = (f32[32,9216]{1,0:T(8,128)S(1)}, f32[32,9216]{1,0:T(8,128)S(1)}, u32[]{:S(2)}, u32[]{:S(2)}) collective-permute-start(f32[32,9216]{1,0:T(8,128)S(1)} %dynamic-slice_subtract_fusion), channel_id=1, source_target_pairs={{0,16},{16,0},{1,17},{17,1},{2,18},{18,2},{3,19},{19,3},{4,20},{20... | collective-permute-start | bytes 3538952 | tf_op jit(solution)/shard_map/ppermute | solution.py:48
where the time goes:
time: 150 us; the launch traced here: 149 us
  blocking collectives  52.4 us (35%)
  waiting for transfers between devices  46.1 us (31%)
  starting transfers between devices  24.5 us (16%)
  matrix products  11.5 us (8%)
  other arithmetic  7.11 us (5%)
  local copies, waits for them, and re-layouts  6.02 us (4%)
  between operations  1.58 us (1%)
    all_to_all x1, blocking collectives, body(): lax.all_to_all(source, 'grp', split_axis=1, concat_axis=0, tiled=True)  35 us
    all_to_all x1, waiting for transfers between devices, body(): lax.all_to_all(update_cols, 'grp', split_axis=0, concat_axis=1, tiled=True)  23.7 us
    all_to_all x2, waiting for transfers between devices, exchange(): return lax.all_to_all(x, 'grp', split_axis=0, concat_axis=0, tiled=True)  19.9 us
    all_to_all x1, blocking collectives, exchange(): return lax.all_to_all(x, 'grp', split_axis=0, concat_axis=0, tiled=True)  17.3 us
    dot_general x11, matrix products, exact_dot(): jnp.dot(left, right, precision=lax.Precision.HIGHEST, preferred_element_t...  11.5 us
    all_to_all x2, starting transfers between devices, exchange(): return lax.all_to_all(x, 'grp', split_axis=0, concat_axis=0, tiled=True)  11.3 us
    ppermute x6, starting transfers between devices, swapped(): return lax.ppermute(x, 'rep', swap)  8.15 us
    all_to_all x1, starting transfers between devices, body(): lax.all_to_all(update_cols, 'grp', split_axis=0, concat_axis=1, tiled=True)  5.05 us
  transfers between devices with their start and end apart: 9, of which 5 were waited for; matrix products, arithmetic and copies ran while one was open for 11% of the time, Pallas kernels for 0%

commit v1 on v0

--- a/solution.py
+++ b/solution.py
@@ -1,3 +1,4 @@
+import functools
 import jax
 import jax.numpy as jnp
 from jax import lax
@@ -9,6 +10,21 @@
 learn_rate = 0.1
 galore_scale = 0.25
 adam_eps = 1e-08
+
+
+def desk_recast(field, axis_k, in_dim):
+    return jnp.concatenate(
+        lax.all_to_all(
+            jnp.stack(jnp.split(field, lax.psum(1, axis_name="grp"), axis=axis_k), axis=0),
+            axis_name="grp",
+            split_axis=0,
+            concat_axis=0,
+        ),
+        axis=in_dim,
+    )
+
+
+keep_up_digits = functools.partial(desk_recast, axis_k=0, in_dim=1)
 
 
 def exact_dot(left, right):
@@ -74,7 +90,7 @@
     gram = gram_half + swapped(gram_half)
     subspace = joined(sub_half, swapped(sub_half))
     update_cols = exact_dot(half_basis, direction.T)
-    update = lax.all_to_all(update_cols, "grp", split_axis=0, concat_axis=1, tiled=True)
+    update = keep_up_digits(update_cols)
     new_half = own_half(weights) - learn_rate * galore_scale * update
     new_weights = joined(new_half, swapped(new_half))
     scale = jnp.sqrt(jnp.sqrt(jnp.sum(gram * gram) + 1e-06))

time: 150 us -> 163 us (1.087)
  local copies, waits for them, and re-layouts: 6.02 us -> 31.2 us
  blocking collectives: 52.4 us -> 35 us
  starting transfers between devices: 24.5 us -> 30.1 us
  matrix products: 11.5 us -> 9.77 us
    all_to_all x1 -> x0, blocking collectives: 17.3 us -> none  [exchange(): return lax.all_to_all(x, 'grp', split_axis=0, concat_axis=0, tiled=True)]
    another operation x0 -> x18, local copies, waits for them, and re-layouts: none -> 15.5 us  [desk_recast(): jnp.stack(jnp.split(field, lax.psum(1, axis_name='grp'), axis=axis_k), ax...]
    unnamed x20 -> x51, local copies, waits for them, and re-layouts: 0.84 us -> 10.5 us
    all_to_all x2 -> x3, starting transfers between devices: 11.3 us -> 17.4 us  [exchange(): return lax.all_to_all(x, 'grp', split_axis=0, concat_axis=0, tiled=True)]
    dot_general x11, matrix products: 11.5 us -> 9.77 us  [exact_dot(): jnp.dot(left, right, precision=lax.Precision.HIGHEST, preferred_element_t...]
    all_to_all x2 -> x3, waiting for transfers between devices: 19.9 us -> 19.5 us  [exchange(): return lax.all_to_all(x, 'grp', split_axis=0, concat_axis=0, tiled=True)]
  transfers between devices with their start and end apart: 9 -> 10, of which waited for: 5 -> 5; matrix products, arithmetic and copies ran while one was open for 11% -> 24% of each run, Pallas kernels for 0% -> 0%
where the time goes in v1:
time: 163 us; the launch traced here: 162 us
  waiting for transfers between devices  47.1 us (29%)
  blocking collectives  35 us (21%)
  local copies, waits for them, and re-layouts  31.2 us (19%)
  starting transfers between devices  30.1 us (18%)
  matrix products  9.77 us (6%)
  other arithmetic  7.29 us (4%)
    all_to_all x1, blocking collectives, body(): lax.all_to_all(source, 'grp', split_axis=1, concat_axis=0, tiled=True)  35 us
    all_to_all x1, waiting for transfers between devices, desk_recast(): lax.all_to_all(jnp.stack(jnp.split(field, lax.psum(1, axis_name='grp'), a...  25.1 us
    all_to_all x3, waiting for transfers between devices, exchange(): return lax.all_to_all(x, 'grp', split_axis=0, concat_axis=0, tiled=True)  19.5 us
    all_to_all x3, starting transfers between devices, exchange(): return lax.all_to_all(x, 'grp', split_axis=0, concat_axis=0, tiled=True)  17.4 us
    another operation x18, local copies, waits for them, and re-layouts, desk_recast(): jnp.stack(jnp.split(field, lax.psum(1, axis_name='grp'), axis=axis_k), ax...  15.5 us
    unnamed x51, local copies, waits for them, and re-layouts  10.5 us
    dot_general x11, matrix products, exact_dot(): jnp.dot(left, right, precision=lax.Precision.HIGHEST, preferred_element_t...  9.77 us
    ppermute x6, starting transfers between devices, swapped(): return lax.ppermute(x, 'rep', swap)  7.99 us
  transfers between devices with their start and end apart: 10, of which 5 were waited for; matrix products, arithmetic and copies ran while one was open for 24% of the time, Pallas kernels for 0%

profile of v1, /device:TPU:9, one launch (start us, length us, event | category | flops | bytes accessed | tf_op | source)
XLA Modules:
  0.0 162.1 jit_solution(6625808407353334620)
XLA Ops:
  0.7 1.4 dynamic-slice_bitcast_fusion
  2.0 0.7 collective-permute-start
  2.8 0.8 tile.4
  3.6 6.7 %all-to-all-start = ((f32[16,32,256]{2,1,0:T(8,128)}), f32[16,32,256]{2,1,0:T(8,128)S(1)}, u32[]{:S(2)}, u32[]{:S(2)}) async-start(f32[16,32,256]{2,1,0:T(8,128)} %tile.4), calls=%async_computation | async-start | bytes 1048576 | tf_op jit(solution)/shard_map/all_to_all | solution.py:72
  10.3 1.4 bitcast_add_fusion
  12.6 11.6 %all-to-all-done = f32[16,32,256]{2,1,0:T(8,128)S(1)} async-done(((f32[16,32,256]{2,1,0:T(8,128)}), f32[16,32,256]{2,1,0:T(8,128)S(1)}, u32[]{:S(2)}, u32[]{:S(2)}) %all-to-all-start) | async-done | bytes 524320 | tf_op jit(solution)/shard_map/all_to_all | solution.py:72
  24.2 35.0 %all_to_all.42 = f32[32,16,576]{2,0,1:T(8,128)S(1)} all-to-all(f32[32,16,576]{2,0,1:T(8,128)S(1)} %copy.36), channel_id=1, replica_groups=mesh['rep'=2,'grp'=16] {'grp'}, dimensions={1} | all-to-all | bytes 2359296 | tf_op jit(solution)/shard_map/all_to_all | solution.py:80
  59.2 2.2 %fusion.4 = f32[576,256]{1,0:T(8,128)S(1)} fusion(f32[16,32,256]{2,1,0:T(8,128)S(1)} %all-to-all-done, f32[32,16,576]{2,0,1:T(8,128)S(1)} %all_to_all.42), kind=kOutput, calls=%fused_computation.6 | convolution fusion | flops 905969664 | bytes 2293760 | tf_op jit(solution)/shard_map/dot_general | solution.py:31
  61.5 2.0 %collective-permute-start.1 = (f32[576,256]{1,0:T(8,128)S(1)}, f32[576,256]{1,0:T(8,128)S(1)}, u32[]{:S(2)}, u32[]{:S(2)}) collective-permute-start(f32[576,256]{1,0:T(8,128)S(1)} %fusion.4), channel_id=1, source_target_pairs={{0,16},{16,0},{1,17},{17,1},{2,18},{18,2},{3,19},{19,3},{4,20},{20... | collective-permute-start | bytes 1769480 | tf_op jit(solution)/shard_map/ppermute | solution.py:64
  63.5 1.6 %collective-permute-done.1 = f32[576,256]{1,0:T(8,128)S(1)} collective-permute-done((f32[576,256]{1,0:T(8,128)S(1)}, f32[576,256]{1,0:T(8,128)S(1)}, u32[]{:S(2)}, u32[]{:S(2)}) %collective-permute-start.1) | collective-permute-done | bytes 589856 | tf_op jit(solution)/shard_map/ppermute | solution.py:64
  65.1 2.2 %fusion = f32[16,32,256]{2,1,0:T(8,128)} fusion(f32[32,16,576]{2,0,1:T(8,128)S(1)} %all_to_all.42, f32[576,256]{1,0:T(8,128)S(1)} %fusion.4, f32[576,256]{1,0:T(8,128)S(1)} %collective-permute-done.1), kind=kOutput, calls=%fused_computation.1 | convolution fusion | flops 906117120 | bytes 2883584 | tf_op jit(solution)/shard_map/dot_general | solution.py:31
  67.3 4.2 %all-to-all-start.3 = ((f32[16,32,256]{2,1,0:T(8,128)}), f32[16,32,256]{2,1,0:T(8,128)S(1)}, u32[]{:S(2)}, u32[]{:S(2)}) async-start(f32[16,32,256]{2,1,0:T(8,128)} %fusion), calls=%async_computation.3 | async-start | bytes 1048576 | tf_op jit(solution)/shard_map/all_to_all | solution.py:72
  71.5 1.5 multiply_add_fusion
  73.1 0.8 copy-done.2
  73.9 1.4 fusion.13
  75.2 2.3 %slice_bitcast_fusion = (f32[1,32,576]{1,2,0:T(8,128)}, f32[1,32,576]{1,2,0:T(8,128)}, f32[1,32,576]{1,2,0:T(8,128)}, f32[1,32,576]{1,2,0:T(8,128)}, f32[1,32,57...) fusion(f32[512,576]{0,1:T(8,128)S(1)} %fusion.13), kind=kLoop, calls=%fused_computation.32 | loop fusion | bytes 2359296 | tf_op jit(solution)/shard_map/stack | solution.py:18
  77.6 1.8 %copy.52 = f32[1,32,576]{2,1,0:T(8,128)} copy(f32[1,32,576]{1,2,0:T(8,128)} %get-tuple-element.12) | data formatting | bytes 147456 | tf_op jit(solution)/shard_map/stack | solution.py:18
  79.4 1.8 %copy.51 = f32[1,32,576]{2,1,0:T(8,128)} copy(f32[1,32,576]{1,2,0:T(8,128)} %get-tuple-element.13) | data formatting | bytes 147456 | tf_op jit(solution)/shard_map/stack | solution.py:18
  81.1 1.7 %copy.50 = f32[1,32,576]{2,1,0:T(8,128)} copy(f32[1,32,576]{1,2,0:T(8,128)} %get-tuple-element.14) | data formatting | bytes 147456 | tf_op jit(solution)/shard_map/stack | solution.py:18
  82.9 1.7 %copy.49 = f32[1,32,576]{2,1,0:T(8,128)} copy(f32[1,32,576]{1,2,0:T(8,128)} %get-tuple-element.15) | data formatting | bytes 147456 | tf_op jit(solution)/shard_map/stack | solution.py:18
  84.6 1.7 %copy.48 = f32[1,32,576]{2,1,0:T(8,128)} copy(f32[1,32,576]{1,2,0:T(8,128)} %get-tuple-element.16) | data formatting | bytes 147456 | tf_op jit(solution)/shard_map/stack | solution.py:18
  86.3 1.7 %copy.47 = f32[1,32,576]{2,1,0:T(8,128)} copy(f32[1,32,576]{1,2,0:T(8,128)} %get-tuple-element.17) | data formatting | bytes 147456 | tf_op jit(solution)/shard_map/stack | solution.py:18
  88.1 0.8 copy.46
  90.1 0.7 constant_dynamic-update-slice_fusion.15
  90.8 0.6 constant_dynamic-update-slice_fusion.14
  91.4 0.6 constant_dynamic-update-slice_fusion.13
  93.3 0.6 constant_dynamic-update-slice_fusion.10
  94.7 0.9 tile.5
  95.6 6.6 %all-to-all-start.4 = ((f32[16,32,256]{2,1,0:T(8,128)}), f32[16,32,256]{2,1,0:T(8,128)S(1)}, u32[]{:S(2)}, u32[]{:S(2)}) async-start(f32[16,32,256]{2,1,0:T(8,128)} %tile.5), calls=%async_computation.4 | async-start | bytes 1048576 | tf_op jit(solution)/shard_map/all_to_all | solution.py:72
  103.4 0.6 constant_dynamic-update-slice_fusion.6
  104.0 0.6 constant_dynamic-update-slice_fusion.5
  104.7 0.6 constant_dynamic-update-slice_fusion.4
  105.3 0.6 constant_dynamic-update-slice_fusion.3
  106.0 0.6 constant_dynamic-update-slice_fusion.2
  106.6 0.6 constant_dynamic-update-slice_fusion.1
  107.3 0.6 constant_dynamic-update-slice_fusion
  107.9 7.9 %all-to-all-done.4 = f32[16,32,256]{2,1,0:T(8,128)S(1)} async-done(((f32[16,32,256]{2,1,0:T(8,128)}), f32[16,32,256]{2,1,0:T(8,128)S(1)}, u32[]{:S(2)}, u32[]{:S(2)}) %all-to-all-start.4) | async-done | bytes 524320 | tf_op jit(solution)/shard_map/all_to_all | solution.py:72
  115.8 4.6 %all-to-all-start.2 = ((f32[16,32,576]{2,1,0:T(8,128)}), f32[16,32,576]{2,1,0:T(8,128)S(1)}, u32[]{:S(2)}, u32[]{:S(2)}) async-start(f32[16,32,576]{2,1,0:T(8,128)} %constant_dynamic-update-slice_fusion), calls=%async_computation.2 | async-start | bytes 2621440 | tf_op jit(solution)/shard_map/all_to_all | solution.py:17
  120.4 2.0 %collective-permute-start.5 = (f32[2,64]{1,0:T(2,128)S(1)}, f32[2,64]{1,0:T(2,128)S(1)}, u32[]{:S(2)}, u32[]{:S(2)}) collective-permute-start(f32[2,64]{1,0:T(2,128)S(1)} %bitcast.70), channel_id=1, source_target_pairs={{0,16},{16,0},{1,17},{17,1},{2,18},{18,2},{3,19},{19,3},{4,20},{20... | collective-permute-start | bytes 1544 | tf_op jit(solution)/shard_map/ppermute | solution.py:64
  122.5 0.8 collective-permute-done.5
  124.2 1.0 convolution_bitcast_fusion
  125.5 25.1 %all-to-all-done.2 = f32[16,32,576]{2,1,0:T(8,128)S(1)} async-done(((f32[16,32,576]{2,1,0:T(8,128)}), f32[16,32,576]{2,1,0:T(8,128)S(1)}, u32[]{:S(2)}, u32[]{:S(2)}) %all-to-all-start.2) | async-done | bytes 1179680 | tf_op jit(solution)/shard_map/all_to_all | solution.py:17
  150.7 0.8 copy.53
  152.0 1.4 dynamic-slice_subtract_fusion
  153.4 2.6 %collective-permute-start.2 = (f32[32,9216]{1,0:T(8,128)S(1)}, f32[32,9216]{1,0:T(8,128)S(1)}, u32[]{:S(2)}, u32[]{:S(2)}) collective-permute-start(f32[32,9216]{1,0:T(8,128)S(1)} %dynamic-slice_subtract_fusion), channel_id=1, source_target_pairs={{0,16},{16,0},{1,17},{17,1},{2,18},{18,2},{3,19},{19,3},{4,20},{20... | collective-permute-start | bytes 3538952 | tf_op jit(solution)/shard_map/ppermute | solution.py:64
  156.0 0.7 multiply_reduce_fusion
  159.6 0.9 fusion.9
  160.5 1.6 maximum_select_fusion
  (69 shorter events, 9.3 us)
Async XLA Ops:
  0.6 2.2 %copy-start = (f32[64,256]{1,0:T(8,128)S(1)}, f32[64,256]{1,0:T(8,128)}, u32[]{:S(2)}) copy-start(f32[64,256]{1,0:T(8,128)} %param.12) | copy-start | bytes 196612
  2.0 8.3 %collective-permute-start = (f32[32,9216]{1,0:T(8,128)S(1)}, f32[32,9216]{1,0:T(8,128)S(1)}, u32[]{:S(2)}, u32[]{:S(2)}) collective-permute-start(f32[32,9216]{1,0:T(8,128)S(1)} %dynamic-slice_bitcast_fusion), channel_id=1, source_target_pairs={{0,16},{16,0},{1,17},{17,1},{2,18},{18,2},{3,19},{19,3},{4,20},{20... | collective-permute-start | bytes 3538952 | tf_op jit(solution)/shard_map/ppermute | solution.py:64
  3.6 20.6 %all-to-all-start = ((f32[16,32,256]{2,1,0:T(8,128)}), f32[16,32,256]{2,1,0:T(8,128)S(1)}, u32[]{:S(2)}, u32[]{:S(2)}) async-start(f32[16,32,256]{2,1,0:T(8,128)} %tile.4), calls=%async_computation | async-start | bytes 1048576 | tf_op jit(solution)/shard_map/all_to_all | solution.py:72
  24.2 35.0 %copy-start.3 = (f32[16,32,256]{2,1,0:T(8,128)}, f32[16,32,256]{2,1,0:T(8,128)S(1)}, u32[]{:S(2)}) copy-start(f32[16,32,256]{2,1,0:T(8,128)S(1)} %all-to-all-done) | copy-start | bytes 1572868
  61.5 3.6 %collective-permute-start.1 = (f32[576,256]{1,0:T(8,128)S(1)}, f32[576,256]{1,0:T(8,128)S(1)}, u32[]{:S(2)}, u32[]{:S(2)}) collective-permute-start(f32[576,256]{1,0:T(8,128)S(1)} %fusion.4), channel_id=1, source_target_pairs={{0,16},{16,0},{1,17},{17,1},{2,18},{18,2},{3,19},{19,3},{4,20},{20... | collective-permute-start | bytes 1769480 | tf_op jit(solution)/shard_map/ppermute | solution.py:64
  67.3 27.3 %all-to-all-start.3 = ((f32[16,32,256]{2,1,0:T(8,128)}), f32[16,32,256]{2,1,0:T(8,128)S(1)}, u32[]{:S(2)}, u32[]{:S(2)}) async-start(f32[16,32,256]{2,1,0:T(8,128)} %fusion), calls=%async_computation.3 | async-start | bytes 1048576 | tf_op jit(solution)/shard_map/all_to_all | solution.py:72
  71.5 2.3 %copy-start.4 = (f32[16,32,256]{2,1,0:T(8,128)S(1)}, f32[16,32,256]{2,1,0:T(8,128)}, u32[]{:S(2)}) copy-start(f32[16,32,256]{2,1,0:T(8,128)} %copy-done.3) | copy-start | bytes 1572868
  73.0 0.8 copy-start.2
  73.1 2.2 %copy-start.1 = (f32[576,256]{1,0:T(8,128)}, f32[576,256]{1,0:T(8,128)S(1)}, u32[]{:S(2)}) copy-start(f32[576,256]{1,0:T(8,128)S(1)} %get-tuple-element.28) | copy-start | bytes 1769476
  77.6 11.3 %copy-start.6 = (f32[1,32,576]{1,2,0:T(8,128)S(1)}, f32[1,32,576]{1,2,0:T(8,128)}, u32[]{:S(2)}) copy-start(f32[1,32,576]{1,2,0:T(8,128)} %get-tuple-element.19) | copy-start | bytes 221188
  79.3 9.6 %copy-start.5 = (f32[1,32,576]{1,2,0:T(8,128)S(1)}, f32[1,32,576]{1,2,0:T(8,128)}, u32[]{:S(2)}) copy-start(f32[1,32,576]{1,2,0:T(8,128)} %get-tuple-element.20) | copy-start | bytes 221188
  94.0 9.4 %copy-start.13 = (f32[1,32,576]{2,1,0:T(8,128)S(1)}, f32[1,32,576]{2,1,0:T(8,128)}, u32[]{:S(2)}) copy-start(f32[1,32,576]{2,1,0:T(8,128)} %copy.46) | copy-start | bytes 221188
  94.6 9.4 %copy-start.12 = (f32[1,32,576]{2,1,0:T(8,128)S(1)}, f32[1,32,576]{2,1,0:T(8,128)}, u32[]{:S(2)}) copy-start(f32[1,32,576]{2,1,0:T(8,128)} %copy.47) | copy-start | bytes 221188
  94.6 10.1 %copy-start.11 = (f32[1,32,576]{2,1,0:T(8,128)S(1)}, f32[1,32,576]{2,1,0:T(8,128)}, u32[]{:S(2)}) copy-start(f32[1,32,576]{2,1,0:T(8,128)} %copy.48) | copy-start | bytes 221188
  94.7 10.7 %copy-start.10 = (f32[1,32,576]{2,1,0:T(8,128)S(1)}, f32[1,32,576]{2,1,0:T(8,128)}, u32[]{:S(2)}) copy-start(f32[1,32,576]{2,1,0:T(8,128)} %copy.49) | copy-start | bytes 221188
  94.7 11.3 %copy-start.9 = (f32[1,32,576]{2,1,0:T(8,128)S(1)}, f32[1,32,576]{2,1,0:T(8,128)}, u32[]{:S(2)}) copy-start(f32[1,32,576]{2,1,0:T(8,128)} %copy.50) | copy-start | bytes 221188
  94.7 12.0 %copy-start.8 = (f32[1,32,576]{2,1,0:T(8,128)S(1)}, f32[1,32,576]{2,1,0:T(8,128)}, u32[]{:S(2)}) copy-start(f32[1,32,576]{2,1,0:T(8,128)} %copy.51) | copy-start | bytes 221188
  95.6 11.7 %copy-start.7 = (f32[1,32,576]{2,1,0:T(8,128)S(1)}, f32[1,32,576]{2,1,0:T(8,128)}, u32[]{:S(2)}) copy-start(f32[1,32,576]{2,1,0:T(8,128)} %copy.52) | copy-start | bytes 221188
  95.6 20.2 %all-to-all-start.4 = ((f32[16,32,256]{2,1,0:T(8,128)}), f32[16,32,256]{2,1,0:T(8,128)S(1)}, u32[]{:S(2)}, u32[]{:S(2)}) async-start(f32[16,32,256]{2,1,0:T(8,128)} %tile.5), calls=%async_computation.4 | async-start | bytes 1048576 | tf_op jit(solution)/shard_map/all_to_all | solution.py:72
  107.9 12.5 %copy-start.15 = (f32[1,2,64]{2,1,0:T(2,128)S(1)}, f32[1,2,64]{2,1,0:T(2,128)}, u32[]{:S(2)}) copy-start(f32[1,2,64]{2,1,0:T(2,128)} %param.10) | copy-start | bytes 1540
  107.9 15.4 %copy-start.14 = (f32[2,64]{1,0:T(2,128)S(1)}, f32[2,64]{1,0:T(2,128)}, u32[]{:S(2)}) copy-start(f32[2,64]{1,0:T(2,128)} %param.15) | copy-start | bytes 1540
  107.9 15.4 %copy-start.16 = (f32[2,64]{1,0:T(2,128)S(1)}, f32[2,64]{1,0:T(2,128)}, u32[]{:S(2)}) copy-start(f32[2,64]{1,0:T(2,128)} %param.16) | copy-start | bytes 1540
  107.9 15.4 %copy-start.17 = (f32[2,64]{1,0:T(2,128)S(1)}, f32[2,64]{1,0:T(2,128)}, u32[]{:S(2)}) copy-start(f32[2,64]{1,0:T(2,128)} %param.17) | copy-start | bytes 1540
  115.8 34.8 %all-to-all-start.2 = ((f32[16,32,576]{2,1,0:T(8,128)}), f32[16,32,576]{2,1,0:T(8,128)S(1)}, u32[]{:S(2)}, u32[]{:S(2)}) async-start(f32[16,32,576]{2,1,0:T(8,128)} %constant_dynamic-update-slice_fusion), calls=%async_computation.2 | async-start | bytes 2621440 | tf_op jit(solution)/shard_map/all_to_all | solution.py:17
  120.4 2.8 %collective-permute-start.5 = (f32[2,64]{1,0:T(2,128)S(1)}, f32[2,64]{1,0:T(2,128)S(1)}, u32[]{:S(2)}, u32[]{:S(2)}) collective-permute-start(f32[2,64]{1,0:T(2,128)S(1)} %bitcast.70), channel_id=1, source_target_pairs={{0,16},{16,0},{1,17},{17,1},{2,18},{18,2},{3,19},{19,3},{4,20},{20... | collective-permute-start | bytes 1544 | tf_op jit(solution)/shard_map/ppermute | solution.py:64
  123.9 34.4 %collective-permute-start.3 = (f32[32,256]{1,0:T(8,128)S(1)}, f32[32,256]{1,0:T(8,128)S(1)}, u32[]{:S(2)}, u32[]{:S(2)}) collective-permute-start(f32[32,256]{1,0:T(8,128)S(1)} %reduce_sum.18), channel_id=1, source_target_pairs={{0,16},{16,0},{1,17},{17,1},{2,18},{18,2},{3,19},{19,3},{4,20},{20... | collective-permute-start | bytes 98312 | tf_op jit(solution)/shard_map/ppermute | solution.py:64
  125.3 30.8 %collective-permute-start.4 = (f32[256,256]{1,0:T(8,128)S(1)}, f32[256,256]{1,0:T(8,128)S(1)}, u32[]{:S(2)}, u32[]{:S(2)}) collective-permute-start(f32[256,256]{1,0:T(8,128)S(1)} %convolution_bitcast_fusion), channel_id=1, source_target_pairs={{0,16},{16,0},{1,17},{17,1},{2,18},{18,2},{3,19},{19,3},{4,20},{20... | collective-permute-start | bytes 786440 | tf_op jit(solution)/shard_map/ppermute | solution.py:64
  153.4 7.1 %collective-permute-start.2 = (f32[32,9216]{1,0:T(8,128)S(1)}, f32[32,9216]{1,0:T(8,128)S(1)}, u32[]{:S(2)}, u32[]{:S(2)}) collective-permute-start(f32[32,9216]{1,0:T(8,128)S(1)} %dynamic-slice_subtract_fusion), channel_id=1, source_target_pairs={{0,16},{16,0},{1,17},{17,1},{2,18},{18,2},{3,19},{19,3},{4,20},{20... | collective-permute-start | bytes 3538952 | tf_op jit(solution)/shard_map/ppermute | solution.py:64
